TPU v7x, 256 devices: a whole 4x4x8 slice. The times are simulated.
256 devices in a mesh: corner: 16 (over y, x_lo, core), tm: 16 (over z, x_hi).
Axes of the slice: x: 4 (x_hi: 2, x_lo: 2; x = x_hi * 2 + x_lo), y: 4, z: 8, core: 2. Of those that a mesh axis runs over, the one named last changes fastest.
Arguments:
- signal: bfloat16 [16, 64, 65536], P('corner', None, 'tm'), may hold values from -6 to 6
- dilated_conv_weight: bfloat16 [2, 256, 128], replicated, may hold values from -0.5 to 0.5
- dilated_conv_bias: float32 [2, 256], replicated, may hold values from -3 to 3
- projection_weight: bfloat16 [2, 128, 128], replicated, may hold values from -0.5 to 0.5
- projection_bias: float32 [2, 128], replicated, may hold values from -3 to 3
- cot_top: bfloat16 [16, 64, 65536], P('corner', None, 'tm'), may hold values from -6 to 6
- cot_skip: bfloat16 [16, 64, 65536], P('corner', None, 'tm'), may hold values from -6 to 6
Outputs:
- x_top: bfloat16 [16, 64, 65536], P('corner', None, 'tm')
- skip_sum: bfloat16 [16, 64, 65536], P('corner', None, 'tm')
- grad_input: bfloat16 [16, 64, 65536], P('corner', None, 'tm')
- grad_conv: float32 [2, 256, 128], replicated
- grad_conv_bias: float32 [2, 256], replicated
- grad_out: float32 [2, 128, 128], replicated
- grad_out_bias: float32 [2, 128], replicated
All inputs are finite; a program needn't handle non-finite values.
Results may differ from a plain program's by a relative error of at most 0.0065.
Values may be sent and summed in bfloat16 or wider, within the bound.
No kernel may reach another device: no remote copies, remote signals or barrier semaphores. Data moves between devices by JAX's collectives and lax.ppermute only.
A program may use at most 64 MiB of HBM per device.

v0:
```python
import math
import jax
import jax.numpy as jnp
from jax import lax
from jax.sharding import PartitionSpec as P


def from_behind(block, axis, distance):
    devices = range(lax.axis_size(axis))
    route = [(i - distance, i) for i in devices if i - distance in devices]
    return lax.ppermute(block, axis, route)


def gated_layer_forward(a_in, tap_in, weight, bias, proj, proj_bias, gsize, rsize):
    stacked = jnp.concatenate([tap_in, a_in], axis=1)
    pre_act = (
        jnp.einsum("oc,bct->bot", weight, stacked, preferred_element_type=jnp.float32)
        + bias[None, :, None]
    )
    gate_out = (jnp.tanh(pre_act[:, :gsize]) * jax.nn.sigmoid(pre_act[:, gsize:])).astype(
        jnp.bfloat16
    )
    mixed = (
        jnp.einsum("og,bgt->bot", proj, gate_out, preferred_element_type=jnp.float32)
        + proj_bias[None, :, None]
    )
    next_act = (a_in.astype(jnp.float32) + mixed[:, :rsize]).astype(jnp.bfloat16)
    return (stacked, pre_act, gate_out, next_act, mixed[:, rsize:])


def layer_backward(go_res, go_skip, stacked, pre_act, gate_out, weight, proj, gsize, rsize):
    upper = jnp.concatenate([go_res, go_skip], axis=1)
    grad_proj = jnp.einsum("bot,bgt->og", upper, gate_out, preferred_element_type=jnp.float32)
    grad_pbias = jnp.sum(upper, axis=(0, 2), dtype=jnp.float32)
    grad_gate = jnp.einsum("og,bot->bgt", proj, upper, preferred_element_type=jnp.float32)
    filt_act = jnp.tanh(pre_act[:, :gsize])
    gate_act = jax.nn.sigmoid(pre_act[:, gsize:])
    grad_pre = jnp.concatenate(
        [
            grad_gate * gate_act * (1.0 - filt_act * filt_act),
            grad_gate * filt_act * gate_act * (1.0 - gate_act),
        ],
        axis=1,
    ).astype(jnp.bfloat16)
    grad_weight = jnp.einsum("bot,bct->oc", grad_pre, stacked, preferred_element_type=jnp.float32)
    grad_bias = jnp.sum(grad_pre, axis=(0, 2), dtype=jnp.float32)
    grad_in = jnp.einsum("oc,bot->bct", weight, grad_pre, preferred_element_type=jnp.float32)
    return (
        grad_in[:, :rsize].astype(jnp.bfloat16),
        grad_in[:, rsize:],
        (grad_weight, grad_bias, grad_proj, grad_pbias),
    )


def on_device(
    signal,
    dilated_conv_weight,
    dilated_conv_bias,
    projection_weight,
    projection_bias,
    cot_top,
    cot_skip,
):
    rsize = signal.shape[1]
    gsize = projection_weight.shape[2]
    tap_near = from_behind(signal, "tm", 1)
    (
        lower_saved_state,
        lower_preactivation,
        lower_gated_output,
        middle_layer_input,
        lower_skip_output,
    ) = gated_layer_forward(
        signal,
        tap_near,
        dilated_conv_weight[0],
        dilated_conv_bias[0],
        projection_weight[0],
        projection_bias[0],
        gsize,
        rsize,
    )
    tap_far = from_behind(middle_layer_input, "tm", 2)
    (
        upper_saved_state,
        upper_preactivation,
        upper_gated_output,
        upper_layer_output,
        upper_skip_output,
    ) = gated_layer_forward(
        middle_layer_input,
        tap_far,
        dilated_conv_weight[1],
        dilated_conv_bias[1],
        projection_weight[1],
        projection_bias[1],
        gsize,
        rsize,
    )
    skip_out = (lower_skip_output + upper_skip_output).astype(jnp.bfloat16)
    delayed_gradient_upper, current_gradient_upper, grads_top = layer_backward(
        cot_top,
        cot_skip,
        upper_saved_state,
        upper_preactivation,
        upper_gated_output,
        dilated_conv_weight[1],
        projection_weight[1],
        gsize,
        rsize,
    )
    later_top = from_behind(delayed_gradient_upper, "tm", -2)
    middle_input_gradient = (
        cot_top.astype(jnp.float32) + current_gradient_upper + later_top.astype(jnp.float32)
    ).astype(jnp.bfloat16)
    delayed_gradient_lower, current_gradient_lower, grads_low = layer_backward(
        middle_input_gradient,
        cot_skip,
        lower_saved_state,
        lower_preactivation,
        lower_gated_output,
        dilated_conv_weight[0],
        projection_weight[0],
        gsize,
        rsize,
    )
    later_low = from_behind(delayed_gradient_lower, "tm", -1)
    lower_input_gradient = (
        middle_input_gradient.astype(jnp.float32)
        + current_gradient_lower
        + later_low.astype(jnp.float32)
    ).astype(jnp.bfloat16)
    summed = lax.psum(
        (
            jnp.stack([grads_low[0], grads_top[0]]),
            jnp.stack([grads_low[1], grads_top[1]]),
            jnp.stack([grads_low[2], grads_top[2]]),
            jnp.stack([grads_low[3], grads_top[3]]),
        ),
        ("corner", "tm"),
    )
    count = signal.shape[0] * lax.axis_size("corner") * signal.shape[2] * lax.axis_size("tm")
    scale = 1.0 / math.sqrt(count)
    return (
        upper_layer_output,
        skip_out,
        lower_input_gradient,
        summed[0] * scale,
        summed[1] * scale,
        summed[2] * scale,
        summed[3] * scale,
    )


def solution(mesh):
    return jax.shard_map(
        on_device,
        mesh=mesh,
        in_specs=(
            P("corner", None, "tm"),
            P(),
            P(),
            P(),
            P(),
            P("corner", None, "tm"),
            P("corner", None, "tm"),
        ),
        out_specs=(
            P("corner", None, "tm"),
            P("corner", None, "tm"),
            P("corner", None, "tm"),
            P(),
            P(),
            P(),
            P(),
        ),
        check_vma=False,
    )
```

profile of v0, /device:TPU:1, one launch (start us, length us, event | category | flops | bytes accessed | tf_op | source)
XLA Modules:
  0.0 411.1 jit_solution(4979422311224916654)
XLA Ops:
  7.2 0.0 all-reduce.4.cloned.1.call-start
  7.2 5.5 %collective-permute-start = (bf16[1,64,4096]{2,1,0:T(8,128)(2,1)}, bf16[1,64,4096]{2,1,0:T(8,128)(2,1)S(1)}, u32[]{:S(2)}, u32[]{:S(2)}) collective-permute-start(bf16[1,64,4096]{2,1,0:T(8,128)(2,1)} %param.7), channel_id=1, source_target_pairs={{0,1},{1,2},{2,3},{3,4},{4,5},{5,6},{6,7},{7,8},{8,9},{9,10},{10,1... | collective-permute-start | bytes 1572872 | tf_op jit(solution)/shard_map/ppermute | solution.py:11
  12.7 0.8 fusion.55
  13.5 0.8 slice_bitcast_fusion
  14.2 1.1 constant_dynamic-update-slice_fusion.1
  15.3 8.3 %collective-permute-done = bf16[1,64,4096]{2,1,0:T(8,128)(2,1)S(1)} collective-permute-done((bf16[1,64,4096]{2,1,0:T(8,128)(2,1)}, bf16[1,64,4096]{2,1,0:T(8,128)(2,1)S(1)}, u32[]{:S(2)}, u32[]{:S(2)}) %collective-permute-start) | collective-permute-done | bytes 524320 | tf_op jit(solution)/shard_map/ppermute | solution.py:11
  23.6 0.0 copy-start.8
  23.6 2.0 fusion.1
  25.6 0.0 copy-done.8
  25.6 0.0 copy-start.10
  25.6 0.8 fusion.18
  26.4 0.0 copy-start.6
  26.4 0.0 copy-done.10
  26.4 0.0 copy-start.5
  26.4 0.4 fusion.5
  26.9 0.6 copy-done.6
  27.5 0.0 copy-start.7
  27.5 0.1 fusion.26
  27.6 5.3 %collective-permute-start.1 = (bf16[1,64,4096]{2,1,0:T(8,128)(2,1)S(1)}, bf16[1,64,4096]{2,1,0:T(8,128)(2,1)S(1)}, u32[]{:S(2)}, u32[]{:S(2)}) collective-permute-start(bf16[1,64,4096]{2,1,0:T(8,128)(2,1)S(1)} %fusion.26), channel_id=1, source_target_pairs={{0,2},{1,3},{2,4},{3,5},{4,6},{5,7},{6,8},{7,9},{8,10},{9,11},{10,... | collective-permute-start | bytes 1572872 | tf_op jit(solution)/shard_map/ppermute | solution.py:11
  32.9 0.0 copy-done.5
  33.0 0.2 convert_reduce_fusion.2
  33.2 9.3 %collective-permute-done.1 = bf16[1,64,4096]{2,1,0:T(8,128)(2,1)S(1)} collective-permute-done((bf16[1,64,4096]{2,1,0:T(8,128)(2,1)S(1)}, bf16[1,64,4096]{2,1,0:T(8,128)(2,1)S(1)}, u32[]{:S(2)}, u32[]{:S(2)}) %collective-permute-start.1) | collective-permute-done | bytes 524320 | tf_op jit(solution)/shard_map/ppermute | solution.py:11
  42.5 0.0 copy-done.7
  42.5 0.7 fusion.3
  43.3 1.5 multiply_convert_fusion.3
  44.8 0.5 convolution_bitcast_fusion.6
  45.3 0.1 slice.203
  45.3 1.3 collective-permute-start.2
  46.6 0.4 fusion.7
  47.0 1.2 fusion.24
  48.3 0.4 convert_reduce_fusion
  48.6 0.7 fusion.16
  49.3 0.0 copy-start.4
  49.3 0.4 convolution_bitcast_fusion.8
  49.8 9.4 %collective-permute-done.2 = bf16[1,64,4096]{2,1,0:T(8,128)(2,1)S(1)} collective-permute-done((bf16[1,64,4096]{2,1,0:T(8,128)(2,1)S(1)}, bf16[1,64,4096]{2,1,0:T(8,128)(2,1)S(1)}, u32[]{:S(2)}, u32[]{:S(2)}) %collective-permute-start.2) | collective-permute-done | bytes 524320 | tf_op jit(solution)/shard_map/ppermute | solution.py:11
  59.2 0.0 copy-done.4
  59.2 0.2 fusion.23
  59.3 1.3 multiply_convert_fusion.1
  60.7 0.0 copy-start
  60.7 0.0 copy-start.2
  60.7 0.2 convert_reduce_fusion.3
  60.9 0.4 convolution_bitcast_fusion.9
  61.4 0.4 convert_reduce_fusion.1
  61.8 0.0 copy-done
  61.8 0.2 copy-done.2
  62.0 82.7 %all-reduce = (f32[2,256]{1,0:T(2,128)S(1)}, f32[2,128]{1,0:T(2,128)S(1)}) all-reduce(f32[2,256]{1,0:T(2,128)S(1)} %pad_maximum_fusion.15, f32[2,128]{1,0:T(2,128)S(1)} %pad_maximum_fusion.16), channel_id=1, replica_groups=mesh['corner'=16,'tm'=16] {'corner','tm'}, use_global_device_ids=true, to_apply=%region_3.0 | all-reduce | flops 768 | bytes 6144 | tf_op jit(solution)/shard_map/psum | solution.py:133
  144.7 0.6 broadcast_multiply_fusion.2
  145.3 0.0 copy-start.1
  145.3 2.2 convolution_bitcast_fusion.4
  147.5 0.8 slice.202
  148.3 1.3 collective-permute-start.3
  149.6 0.7 pad_maximum_fusion.14
  150.3 0.0 copy-done.1
  150.3 0.0 copy-done.3
  150.3 0.0 copy-done.9
  150.3 0.7 fusion.17
  151.0 0.7 pad_maximum_fusion.13
  151.7 0.0 all-reduce.4.cloned.1.call-update
  151.7 0.6 broadcast_multiply_fusion.3
  152.3 246.7 %all-reduce.4.cloned.1.call-done = (f32[2,256,128]{2,1,0:T(8,128)}, f32[2,128,128]{2,1,0:T(8,128)}) async-done(((f32[2,256,128]{2,1,0:T(8,128)}, f32[2,128,128]{2,1,0:T(8,128)}), (f32[2,256,128]{2,1,0:T(8,128)}, f32[2,128,128]{2,1,0:T(8,128)})) %all-reduce.4.cloned.1.call-update) | async-done | bytes 393232 | tf_op jit(solution)/shard_map/psum | solution.py:133
  399.0 1.6 broadcast_multiply_fusion.1
  400.6 1.7 broadcast_multiply_fusion
  402.2 0.0 collective-permute-done.3
  402.2 2.0 fusion.21
  (5 shorter events, 0.1 us)
Async XLA Ops:
  7.2 391.8 %all-reduce.4.cloned.1.call-start = ((), (), s32[]{:S(2)}) async-start(), calls=%async_computation | async-start | bytes 786432 | tf_op jit(solution)/shard_map/psum | solution.py:133
  7.2 16.4 %collective-permute-start = (bf16[1,64,4096]{2,1,0:T(8,128)(2,1)}, bf16[1,64,4096]{2,1,0:T(8,128)(2,1)S(1)}, u32[]{:S(2)}, u32[]{:S(2)}) collective-permute-start(bf16[1,64,4096]{2,1,0:T(8,128)(2,1)} %param.7), channel_id=1, source_target_pairs={{0,1},{1,2},{2,3},{3,4},{4,5},{5,6},{6,7},{7,8},{8,9},{9,10},{10,1... | collective-permute-start | bytes 1572872 | tf_op jit(solution)/shard_map/ppermute | solution.py:11
  23.6 2.0 copy-start.8
  25.6 0.9 copy-start.10
  26.4 1.0 copy-start.6
  26.4 6.5 %copy-start.5 = (bf16[1,64,4096]{2,1,0:T(8,128)(2,1)S(1)}, bf16[1,64,4096]{2,1,0:T(8,128)(2,1)}, u32[]{:S(2)}) copy-start(bf16[1,64,4096]{2,1,0:T(8,128)(2,1)} %param.13) | copy-start | bytes 1572868
  27.5 15.1 %copy-start.7 = (bf16[2,256,128]{2,1,0:T(8,128)(2,1)S(1)}, bf16[2,256,128]{2,1,0:T(8,128)(2,1)}, u32[]{:S(2)}) copy-start(bf16[2,256,128]{2,1,0:T(8,128)(2,1)} %param.8) | copy-start | bytes 393220
  27.6 15.0 %collective-permute-start.1 = (bf16[1,64,4096]{2,1,0:T(8,128)(2,1)S(1)}, bf16[1,64,4096]{2,1,0:T(8,128)(2,1)S(1)}, u32[]{:S(2)}, u32[]{:S(2)}) collective-permute-start(bf16[1,64,4096]{2,1,0:T(8,128)(2,1)S(1)} %fusion.26), channel_id=1, source_target_pairs={{0,2},{1,3},{2,4},{3,5},{4,6},{5,7},{6,8},{7,9},{8,10},{9,11},{10,... | collective-permute-start | bytes 1572872 | tf_op jit(solution)/shard_map/ppermute | solution.py:11
  45.3 13.9 %collective-permute-start.2 = (bf16[1,64,4096]{2,1,0:T(8,128)(2,1)S(1)}, bf16[1,64,4096]{2,1,0:T(8,128)(2,1)S(1)}, u32[]{:S(2)}, u32[]{:S(2)}) collective-permute-start(bf16[1,64,4096]{2,1,0:T(8,128)(2,1)S(1)} %slice.203), channel_id=1, source_target_pairs={{2,0},{3,1},{4,2},{5,3},{6,4},{7,5},{8,6},{9,7},{10,8},{11,9},{12,... | collective-permute-start | bytes 1572872 | tf_op jit(solution)/shard_map/ppermute | solution.py:11
  49.3 9.8 %copy-start.4 = (bf16[1,64,4096]{2,1,0:T(8,128)(2,1)S(1)}, bf16[1,64,4096]{2,1,0:T(8,128)(2,1)}, u32[]{:S(2)}) copy-start(bf16[1,64,4096]{2,1,0:T(8,128)(2,1)} %param.12) | copy-start | bytes 1572868
  60.7 1.1 copy-start
  60.7 1.3 copy-start.2
  145.3 5.0 %copy-start.1 = (bf16[1,128,4096]{2,1,0:T(8,128)(2,1)S(1)}, bf16[1,128,4096]{2,1,0:T(8,128)(2,1)}, u32[]{:S(2)}) copy-start(bf16[1,128,4096]{2,1,0:T(8,128)(2,1)} %copy-done) | copy-start | bytes 3145732
  145.3 5.0 %copy-start.3 = (bf16[1,128,4096]{2,1,0:T(8,128)(2,1)S(1)}, bf16[1,128,4096]{2,1,0:T(8,128)(2,1)}, u32[]{:S(2)}) copy-start(bf16[1,128,4096]{2,1,0:T(8,128)(2,1)} %copy-done.2) | copy-start | bytes 3145732
  145.3 5.0 %copy-start.9 = (bf16[1,64,4096]{2,1,0:T(8,128)(2,1)S(1)}, bf16[1,64,4096]{2,1,0:T(8,128)(2,1)}, u32[]{:S(2)}) copy-start(bf16[1,64,4096]{2,1,0:T(8,128)(2,1)} %copy-done.8) | copy-start | bytes 1572868
  148.3 253.9 %collective-permute-start.3 = (bf16[1,64,4096]{2,1,0:T(8,128)(2,1)}, bf16[1,64,4096]{2,1,0:T(8,128)(2,1)}, u32[]{:S(2)}, u32[]{:S(2)}) collective-permute-start(bf16[1,64,4096]{2,1,0:T(8,128)(2,1)} %slice.202), channel_id=1, source_target_pairs={{1,0},{2,1},{3,2},{4,3},{5,4},{6,5},{7,6},{8,7},{9,8},{10,9},{11,1... | collective-permute-start | bytes 1572872 | tf_op jit(solution)/shard_map/ppermute | solution.py:11
Sparse Core Ops, SparseCore 0:
  151.9 247.0 all-reduce.3
where the time goes:
time: 412 us; the launch traced here: 411 us
  waiting for transfers between devices  274 us (67%)
  blocking collectives  82.7 us (20%)
  between operations  14.3 us (3%)
  starting transfers between devices  13.5 us (3%)
  matrix products  11.3 us (3%)
  other arithmetic  11.3 us (3%)
  local copies, waits for them, and re-layouts  4.41 us (1%)
    psum x1, waiting for transfers between devices, on_device(): lax.psum((jnp.stack([grads_low[0], grads_top[0]]), jnp.stack([grads_low[1...  247 us
    psum x1, blocking collectives, on_device(): lax.psum((jnp.stack([grads_low[0], grads_top[0]]), jnp.stack([grads_low[1...  82.7 us
    ppermute x4, waiting for transfers between devices, from_behind(): return lax.ppermute(block, axis, route)  27 us
    ppermute x4, starting transfers between devices, from_behind(): return lax.ppermute(block, axis, route)  13.4 us
  transfers between devices with their start and end apart: 5, of which 4 were waited for; matrix products, arithmetic and copies ran while one was open for 3% of the time, Pallas kernels for 0%

commit v1 on v0

--- a/solution.py
+++ b/solution.py
@@ -131,13 +131,16 @@
         + later_low.astype(jnp.float32)
     ).astype(jnp.bfloat16)
     summed = lax.psum(
-        (
-            jnp.stack([grads_low[0], grads_top[0]]),
-            jnp.stack([grads_low[1], grads_top[1]]),
-            jnp.stack([grads_low[2], grads_top[2]]),
-            jnp.stack([grads_low[3], grads_top[3]]),
+        lax.psum(
+            (
+                jnp.stack([grads_low[0], grads_top[0]]),
+                jnp.stack([grads_low[1], grads_top[1]]),
+                jnp.stack([grads_low[2], grads_top[2]]),
+                jnp.stack([grads_low[3], grads_top[3]]),
+            ),
+            "tm",
         ),
-        ("corner", "tm"),
+        "corner",
     )
     count = signal.shape[0] * lax.axis_size("corner") * signal.shape[2] * lax.axis_size("tm")
     scale = 1.0 / math.sqrt(count)

time: 412 us -> 368 us (0.89)
  waiting for transfers between devices: 274 us -> 240 us
  blocking collectives: 82.7 us -> 75.9 us
    psum x1, waiting for transfers between devices: 247 us -> 80.3 us  [on_device(): lax.psum((jnp.stack([grads_low[0], grads_top[0]]), jnp.stack([grads_low[1...]
    psum x0 -> x1, waiting for transfers between devices: none -> 133 us  [on_device(): lax.psum(lax.psum((jnp.stack([grads_low[0], grads_top[0]]), jnp.stack([gr...]
    psum x1, blocking collectives: 82.7 us -> 39.2 us  [on_device(): lax.psum((jnp.stack([grads_low[0], grads_top[0]]), jnp.stack([grads_low[1...]
    psum x0 -> x1, blocking collectives: none -> 36.7 us  [on_device(): lax.psum(lax.psum((jnp.stack([grads_low[0], grads_top[0]]), jnp.stack([gr...]
  transfers between devices with their start and end apart: 5 -> 6, of which waited for: 4 -> 5; matrix products, arithmetic and copies ran while one was open for 3% -> 3% of each run, Pallas kernels for 0% -> 0%
where the time goes in v1:
time: 368 us; the launch traced here: 367 us
  waiting for transfers between devices  240 us (65%)
  blocking collectives  75.9 us (21%)
  between operations  14.3 us (4%)
  starting transfers between devices  13.5 us (4%)
  other arithmetic  10.2 us (3%)
  matrix products  9.4 us (3%)
  local copies, waits for them, and re-layouts  4.14 us (1%)
    psum x1, waiting for transfers between devices, on_device(): lax.psum(lax.psum((jnp.stack([grads_low[0], grads_top[0]]), jnp.stack([gr...  133 us
    psum x1, waiting for transfers between devices, on_device(): lax.psum((jnp.stack([grads_low[0], grads_top[0]]), jnp.stack([grads_low[1...  80.3 us
    psum x1, blocking collectives, on_device(): lax.psum((jnp.stack([grads_low[0], grads_top[0]]), jnp.stack([grads_low[1...  39.2 us
    psum x1, blocking collectives, on_device(): lax.psum(lax.psum((jnp.stack([grads_low[0], grads_top[0]]), jnp.stack([gr...  36.7 us
    ppermute x4, waiting for transfers between devices, from_behind(): return lax.ppermute(block, axis, route)  27 us
    ppermute x4, starting transfers between devices, from_behind(): return lax.ppermute(block, axis, route)  13.4 us
  transfers between devices with their start and end apart: 6, of which 5 were waited for; matrix products, arithmetic and copies ran while one was open for 3% of the time, Pallas kernels for 0%

profile of v1, /device:TPU:1, one launch (start us, length us, event | category | flops | bytes accessed | tf_op | source)
XLA Modules:
  0.0 367.5 jit_solution(3252384787430136955)
XLA Ops:
  7.2 0.0 all-reduce.7.cloned.1.call-start
  7.2 5.5 %collective-permute-start = (bf16[1,64,4096]{2,1,0:T(8,128)(2,1)}, bf16[1,64,4096]{2,1,0:T(8,128)(2,1)S(1)}, u32[]{:S(2)}, u32[]{:S(2)}) collective-permute-start(bf16[1,64,4096]{2,1,0:T(8,128)(2,1)} %param.7), channel_id=1, source_target_pairs={{0,1},{1,2},{2,3},{3,4},{4,5},{5,6},{6,7},{7,8},{8,9},{9,10},{10,1... | collective-permute-start | bytes 1572872 | tf_op jit(solution)/shard_map/ppermute | solution.py:11
  12.7 0.8 fusion.55
  13.5 0.8 slice_bitcast_fusion
  14.2 1.1 constant_dynamic-update-slice_fusion.1
  15.3 8.3 %collective-permute-done = bf16[1,64,4096]{2,1,0:T(8,128)(2,1)S(1)} collective-permute-done((bf16[1,64,4096]{2,1,0:T(8,128)(2,1)}, bf16[1,64,4096]{2,1,0:T(8,128)(2,1)S(1)}, u32[]{:S(2)}, u32[]{:S(2)}) %collective-permute-start) | collective-permute-done | bytes 524320 | tf_op jit(solution)/shard_map/ppermute | solution.py:11
  23.6 1.8 fusion.1
  25.4 0.0 copy-start.4
  25.4 0.8 fusion.18
  26.2 0.0 copy-start.2
  26.2 0.0 copy-done.4
  26.2 0.0 copy-start.1
  26.2 0.4 fusion.5
  26.7 0.6 copy-done.2
  27.3 0.0 copy-start.3
  27.3 0.1 fusion.26
  27.4 5.3 %collective-permute-start.1 = (bf16[1,64,4096]{2,1,0:T(8,128)(2,1)S(1)}, bf16[1,64,4096]{2,1,0:T(8,128)(2,1)S(1)}, u32[]{:S(2)}, u32[]{:S(2)}) collective-permute-start(bf16[1,64,4096]{2,1,0:T(8,128)(2,1)S(1)} %fusion.26), channel_id=1, source_target_pairs={{0,2},{1,3},{2,4},{3,5},{4,6},{5,7},{6,8},{7,9},{8,10},{9,11},{10,... | collective-permute-start | bytes 1572872 | tf_op jit(solution)/shard_map/ppermute | solution.py:11
  32.7 0.0 copy-done.1
  32.7 0.2 convert_reduce_fusion.2
  33.0 9.3 %collective-permute-done.1 = bf16[1,64,4096]{2,1,0:T(8,128)(2,1)S(1)} collective-permute-done((bf16[1,64,4096]{2,1,0:T(8,128)(2,1)S(1)}, bf16[1,64,4096]{2,1,0:T(8,128)(2,1)S(1)}, u32[]{:S(2)}, u32[]{:S(2)}) %collective-permute-start.1) | collective-permute-done | bytes 524320 | tf_op jit(solution)/shard_map/ppermute | solution.py:11
  42.3 0.0 copy-done.3
  42.3 0.7 fusion.3
  43.0 1.5 multiply_convert_fusion.3
  44.5 0.5 convolution_bitcast_fusion.6
  45.0 0.1 slice.203
  45.1 1.3 collective-permute-start.2
  46.4 0.4 fusion.7
  46.8 1.2 fusion.24
  48.0 0.4 convert_reduce_fusion
  48.3 0.7 fusion.16
  49.0 0.0 copy-start
  49.1 0.4 convolution_bitcast_fusion.8
  49.5 9.4 %collective-permute-done.2 = bf16[1,64,4096]{2,1,0:T(8,128)(2,1)S(1)} collective-permute-done((bf16[1,64,4096]{2,1,0:T(8,128)(2,1)S(1)}, bf16[1,64,4096]{2,1,0:T(8,128)(2,1)S(1)}, u32[]{:S(2)}, u32[]{:S(2)}) %collective-permute-start.2) | collective-permute-done | bytes 524320 | tf_op jit(solution)/shard_map/ppermute | solution.py:11
  59.0 0.0 copy-done
  59.0 0.2 fusion.23
  59.1 1.3 multiply_convert_fusion.1
  60.5 0.2 convert_reduce_fusion.3
  60.7 0.4 convolution_bitcast_fusion.9
  61.1 0.4 convert_reduce_fusion.1
  61.5 0.5 convolution_bitcast_fusion.4
  62.0 0.8 slice.202
  62.8 1.3 collective-permute-start.3
  64.1 0.7 pad_maximum_fusion.14
  64.8 0.7 fusion.17
  65.5 0.7 pad_maximum_fusion.13
  66.2 0.0 all-reduce.7.cloned.1.call-update
  66.3 0.0 all-reduce.9.cloned.1.call-start
  66.3 39.2 %all-reduce = (f32[2,256]{1,0:T(2,128)S(1)}, f32[2,128]{1,0:T(2,128)S(1)}) all-reduce(f32[2,256]{1,0:T(2,128)S(1)} %pad_maximum_fusion.15, f32[2,128]{1,0:T(2,128)S(1)} %pad_maximum_fusion.16), channel_id=1, replica_groups=mesh['corner'=16,'tm'=16] {'tm'}, use_global_device_ids=true, to_apply=%region_4.0 | all-reduce | flops 768 | bytes 6144 | tf_op jit(solution)/shard_map/psum | solution.py:134
  105.5 36.7 %all-reduce.2 = (f32[2,256]{1,0:T(2,128)S(1)}, f32[2,128]{1,0:T(2,128)S(1)}) all-reduce(f32[2,256]{1,0:T(2,128)S(1)} %get-tuple-element.7, f32[2,128]{1,0:T(2,128)S(1)} %get-tuple-element.8), channel_id=1, replica_groups=mesh['corner'=16,'tm'=16] {'corner'}, use_global_device_ids=true, to_apply=%region_5.0 | all-reduce | flops 768 | bytes 6144 | tf_op jit(solution)/shard_map/psum | solution.py:133
  142.2 0.6 broadcast_multiply_fusion.3
  142.8 0.6 broadcast_multiply_fusion.2
  143.4 80.3 %all-reduce.7.cloned.1.call-done = (f32[2,256,128]{2,1,0:T(8,128)}, f32[2,128,128]{2,1,0:T(8,128)}) async-done(((f32[2,256,128]{2,1,0:T(8,128)}, f32[2,128,128]{2,1,0:T(8,128)}), (f32[2,256,128]{2,1,0:T(8,128)}, f32[2,128,128]{2,1,0:T(8,128)})) %all-reduce.7.cloned.1.call-update) | async-done | bytes 393232 | tf_op jit(solution)/shard_map/psum | solution.py:134
  223.7 0.0 all-reduce.9.cloned.1.call-update
  223.7 0.0 collective-permute-done.3
  223.7 1.0 fusion.21
  224.7 132.7 %all-reduce.9.cloned.1.call-done = (f32[2,256,128]{2,1,0:T(8,128)}, f32[2,128,128]{2,1,0:T(8,128)}) async-done(((f32[2,256,128]{2,1,0:T(8,128)}, f32[2,128,128]{2,1,0:T(8,128)}), (f32[2,256,128]{2,1,0:T(8,128)}, f32[2,128,128]{2,1,0:T(8,128)})) %all-reduce.9.cloned.1.call-update) | async-done | bytes 393232 | tf_op jit(solution)/shard_map/psum | solution.py:133
  357.4 1.7 broadcast_multiply_fusion
  359.1 1.6 broadcast_multiply_fusion.1
  (3 shorter events, 0.1 us)
Async XLA Ops:
  7.2 216.5 %all-reduce.7.cloned.1.call-start = ((), (), s32[]{:S(2)}) async-start(), calls=%async_computation | async-start | bytes 786432 | tf_op jit(solution)/shard_map/psum | solution.py:134
  7.2 16.4 %collective-permute-start = (bf16[1,64,4096]{2,1,0:T(8,128)(2,1)}, bf16[1,64,4096]{2,1,0:T(8,128)(2,1)S(1)}, u32[]{:S(2)}, u32[]{:S(2)}) collective-permute-start(bf16[1,64,4096]{2,1,0:T(8,128)(2,1)} %param.7), channel_id=1, source_target_pairs={{0,1},{1,2},{2,3},{3,4},{4,5},{5,6},{6,7},{7,8},{8,9},{9,10},{10,1... | collective-permute-start | bytes 1572872 | tf_op jit(solution)/shard_map/ppermute | solution.py:11
  25.4 0.9 copy-start.4
  26.2 1.0 copy-start.2
  26.2 6.5 %copy-start.1 = (bf16[1,64,4096]{2,1,0:T(8,128)(2,1)S(1)}, bf16[1,64,4096]{2,1,0:T(8,128)(2,1)}, u32[]{:S(2)}) copy-start(bf16[1,64,4096]{2,1,0:T(8,128)(2,1)} %param.13) | copy-start | bytes 1572868
  27.3 15.1 %copy-start.3 = (bf16[2,256,128]{2,1,0:T(8,128)(2,1)S(1)}, bf16[2,256,128]{2,1,0:T(8,128)(2,1)}, u32[]{:S(2)}) copy-start(bf16[2,256,128]{2,1,0:T(8,128)(2,1)} %param.8) | copy-start | bytes 393220
  27.4 15.0 %collective-permute-start.1 = (bf16[1,64,4096]{2,1,0:T(8,128)(2,1)S(1)}, bf16[1,64,4096]{2,1,0:T(8,128)(2,1)S(1)}, u32[]{:S(2)}, u32[]{:S(2)}) collective-permute-start(bf16[1,64,4096]{2,1,0:T(8,128)(2,1)S(1)} %fusion.26), channel_id=1, source_target_pairs={{0,2},{1,3},{2,4},{3,5},{4,6},{5,7},{6,8},{7,9},{8,10},{9,11},{10,... | collective-permute-start | bytes 1572872 | tf_op jit(solution)/shard_map/ppermute | solution.py:11
  45.1 13.9 %collective-permute-start.2 = (bf16[1,64,4096]{2,1,0:T(8,128)(2,1)S(1)}, bf16[1,64,4096]{2,1,0:T(8,128)(2,1)S(1)}, u32[]{:S(2)}, u32[]{:S(2)}) collective-permute-start(bf16[1,64,4096]{2,1,0:T(8,128)(2,1)S(1)} %slice.203), channel_id=1, source_target_pairs={{2,0},{3,1},{4,2},{5,3},{6,4},{7,5},{8,6},{9,7},{10,8},{11,9},{12,... | collective-permute-start | bytes 1572872 | tf_op jit(solution)/shard_map/ppermute | solution.py:11
  49.0 9.9 %copy-start = (bf16[1,64,4096]{2,1,0:T(8,128)(2,1)S(1)}, bf16[1,64,4096]{2,1,0:T(8,128)(2,1)}, u32[]{:S(2)}) copy-start(bf16[1,64,4096]{2,1,0:T(8,128)(2,1)} %param.12) | copy-start | bytes 1572868
  62.8 160.9 %collective-permute-start.3 = (bf16[1,64,4096]{2,1,0:T(8,128)(2,1)}, bf16[1,64,4096]{2,1,0:T(8,128)(2,1)S(1)}, u32[]{:S(2)}, u32[]{:S(2)}) collective-permute-start(bf16[1,64,4096]{2,1,0:T(8,128)(2,1)} %slice.202), channel_id=1, source_target_pairs={{1,0},{2,1},{3,2},{4,3},{5,4},{6,5},{7,6},{8,7},{9,8},{10,9},{11,1... | collective-permute-start | bytes 1572872 | tf_op jit(solution)/shard_map/ppermute | solution.py:11
  66.3 291.1 %all-reduce.9.cloned.1.call-start = ((), (), s32[]{:S(2)}) async-start(), calls=%async_computation.1 | async-start | bytes 786432 | tf_op jit(solution)/shard_map/psum | solution.py:133
Sparse Core Ops, SparseCore 0:
  66.4 157.2 all-reduce.6
  226.5 130.8 all-reduce.8
